TPU v7x, 32 devices: a whole 2x2x4 slice. The times are simulated.
32 devices in a mesh: group: 8 (over y, x, core), tp: 4 (over z).
Axes of the slice: x: 2, y: 2, z: 4, core: 2. Of those that a mesh axis runs over, the one named last changes fastest.
Arguments:
- hidden: bfloat16 [2048, 8192], P('group', 'tp'), may hold values from -6 to 6
- w_kv: bfloat16 [8192, 2048], P('tp'), may hold values from -0.0625 to 0.0625
- prompt_lengths: int32 [2, 8], replicated, may hold values from 1 to 128, 256 in all within a row
- owner_step: int32 [2, 8], replicated, may hold values from 1 to 3
- cache: bfloat16 [64, 128, 2048], P(('group', 'tp')), may hold values from -8 to 8
- cache_len: int32 [64], P(('group', 'tp')), may hold values from 1 to 128
- queries: bfloat16 [64, 8192], P('group', 'tp'), may hold values from -200 to 200
- fresh: bfloat16 [64, 2048], P('group', 'tp'), may hold values from -10 to 10
- logits: bfloat16 [64, 30720], P('group', 'tp'), may hold values from -300 to 300
- states: int32 [64], P('group'), may hold values from 0 to 23
- masks: int32 [24, 1024], P(None, 'tp'), may hold values from 0 to 1073741823, as said below
Outputs:
- attended: bfloat16 [64, 8192], P('group', 'tp')
- logprob: float32 [64, 30720], P('group', 'tp')
Inputs may be any that keep to these rules, and one draw needn't show every extreme that they name: `prompt_lengths`: each row sums to 256; the longest prompt of every row has exactly 128 tokens. Prompt k of prefill group p goes to group p + owner_step[p, k] * 2. `masks`: every state allows at least one token in each aligned block of 7680 vocabulary entries.
All inputs are finite; a program needn't handle non-finite values.
Results may differ from a plain program's by a relative error of at most 0.02.
Values may be sent and summed in bfloat16 or wider, within the bound.
A program may use at most 64 MiB of HBM per device.

v0:
```python
import math

import jax
import jax.numpy as jnp
from jax import lax
from jax.sharding import PartitionSpec as P

HEADS = 64
KVH = 8
HD = 128
MAXLEN = 128
CACHE = 128
STATES = 24


def from_behind(block, axis, distance):
    devices = range(lax.axis_size(axis))
    route = [(i - distance, i) for i in devices if i - distance in devices]
    return lax.ppermute(block, axis, route)


def landing(slot_ids, source, turn_index, prompt_lengths, owner_step):
    chosen = owner_step[source] == turn_index
    ranking = jnp.cumsum(chosen.astype(jnp.int32)) - 1
    arrivals = jnp.sum(chosen.astype(jnp.int32))
    matched = chosen[None, :] & (ranking[None, :] == slot_ids[:, None])
    lengths = prompt_lengths[source]
    starts = jnp.cumsum(lengths) - lengths
    first_row = jnp.sum(jnp.where(matched, starts[None, :], 0), axis=1)
    prompt_len = jnp.sum(jnp.where(matched, lengths[None, :], 0), axis=1)
    landed = (slot_ids < arrivals) & (turn_index >= 1)
    return (landed, first_row, prompt_len)


def attend(query_rows, merged, alive_len, fresh_rows):
    row_count = merged.shape[0]
    group_size = HEADS // KVH
    key_rows = merged[:, :, : KVH * HD].reshape(row_count, CACHE, KVH, HD)
    value_rows = merged[:, :, KVH * HD :].reshape(row_count, CACHE, KVH, HD)
    queries = query_rows.reshape(row_count, KVH, group_size, HD)
    own_key = fresh_rows[:, : KVH * HD].reshape(row_count, KVH, HD)
    own_value = fresh_rows[:, KVH * HD :].reshape(row_count, KVH, HD)
    scaling = 1.0 / math.sqrt(HD)
    scores = (
        jnp.einsum("rkgd,rtkd->rkgt", queries, key_rows, preferred_element_type=jnp.float32)
        * scaling
    )
    own_score = (
        jnp.einsum("rkgd,rkd->rkg", queries, own_key, preferred_element_type=jnp.float32) * scaling
    )
    positions = jnp.arange(CACHE, dtype=jnp.int32)
    alive_mask = (positions[None, :] < alive_len[:, None])[:, None, None, :]
    highest = jnp.maximum(jnp.max(jnp.where(alive_mask, scores, -jnp.inf), axis=3), own_score)
    exponent = jnp.where(alive_mask, jnp.exp(scores - highest[..., None]), 0.0)
    own_exponent = jnp.exp(own_score - highest)
    denominator = jnp.sum(exponent, axis=3) + own_exponent
    weights = (exponent / denominator[..., None]).astype(jnp.bfloat16)
    own_weight = (own_exponent / denominator).astype(jnp.bfloat16)
    attended = jnp.einsum(
        "rkgt,rtkd->rkgd", weights, value_rows, preferred_element_type=jnp.float32
    )
    attended = (
        attended
        + own_weight.astype(jnp.float32)[..., None] * own_value.astype(jnp.float32)[:, :, None, :]
    )
    return attended.reshape(row_count, HEADS * HD).astype(jnp.bfloat16)


def per_device(
    hidden,
    w_kv,
    prompt_lengths,
    owner_step,
    cache,
    cache_len,
    queries,
    fresh,
    logits,
    states,
    masks,
):
    tensor_size = lax.axis_size("tp")
    groups = lax.axis_size("group")
    prefill = groups // 4
    group_index = lax.axis_index("group")
    column = lax.axis_index("tp")
    is_prefill = group_index < prefill
    source = group_index % prefill
    turn_index = group_index // prefill
    token_count = hidden.shape[0]
    kv_width = w_kv.shape[1]
    own_count = cache.shape[0]
    own_slots = jnp.arange(own_count, dtype=jnp.int32) * tensor_size + column
    landed, first_row, prompt_len = landing(
        own_slots, source, turn_index, prompt_lengths, owner_step
    )

    def compute():
        return jnp.dot(hidden, w_kv, preferred_element_type=jnp.float32)

    kv_piece = lax.psum_scatter(
        lax.cond(
            is_prefill,
            compute,
            lambda: jnp.zeros(
                (token_count // tensor_size * lax.axis_size("tp"), kv_width), jnp.float32
            ),
        ).astype(jnp.bfloat16),
        "tp",
        scatter_dimension=0,
        tiled=True,
    )
    arrived = [from_behind(kv_piece, "group", prefill * step_index) for step_index in (1, 2, 3)]
    incoming = jnp.where(
        turn_index == 1, arrived[0], jnp.where(turn_index == 2, arrived[1], arrived[2])
    )
    gathered = lax.all_gather(incoming, "tp", axis=0, tiled=True)
    padded = jnp.pad(gathered, ((0, MAXLEN), (0, 0)))
    handed = jax.vmap(lambda offset: lax.dynamic_slice_in_dim(padded, offset, MAXLEN, 0))(first_row)
    front = jnp.where(landed[:, None, None], handed, cache)
    merged = jnp.concatenate([front, cache[:, MAXLEN:]], axis=1)
    alive_len = jnp.where(landed, prompt_len, cache_len)
    mine_queries, mine_fresh = (
        lax.all_to_all(queries, "tp", split_axis=0, concat_axis=1, tiled=True),
        lax.all_to_all(fresh, "tp", split_axis=0, concat_axis=1, tiled=True),
    )
    attended = attend(mine_queries, merged, alive_len, mine_fresh)
    attended = lax.all_to_all(attended, "tp", split_axis=1, concat_axis=0, tiled=True)
    onehot = states[:, None] == jnp.arange(STATES, dtype=jnp.int32)[None, :]
    packed = jnp.sum(jnp.where(onehot[:, :, None], masks[None, :, :], 0), axis=1)
    shifts = jnp.arange(30, dtype=jnp.int32)
    bit_flags = jnp.bitwise_and(jnp.right_shift(packed[:, :, None], shifts[None, None, :]), 1)
    permitted = bit_flags.reshape(packed.shape[0], logits.shape[1]) == 1
    values = logits.astype(jnp.float32)
    local_peak = jnp.max(jnp.where(permitted, values, -jnp.inf), axis=1)
    highest = lax.pmax(local_peak, "tp")
    local_terms = jnp.sum(jnp.where(permitted, jnp.exp(values - highest[:, None]), 0.0), axis=1)
    denominator = lax.psum(local_terms, "tp")
    normalizer = highest + jnp.log(denominator)
    logprob = jnp.where(permitted, values - normalizer[:, None], 0.0)
    return (attended, logprob)


def solution(mesh):
    in_specs = (
        P("group", "tp"),
        P("tp", None),
        P(),
        P(),
        P(("group", "tp"), None, None),
        P(("group", "tp")),
        P("group", "tp"),
        P("group", "tp"),
        P("group", "tp"),
        P("group"),
        P(None, "tp"),
    )
    out_specs = (P("group", "tp"), P("group", "tp"))
    return jax.shard_map(
        per_device, mesh=mesh, in_specs=in_specs, out_specs=out_specs, check_vma=False
    )
```

profile of v0, /device:TPU:4, one launch (start us, length us, event | category | flops | bytes accessed | tf_op | source)
XLA Modules:
  0.0 110.5 jit_solution(17203343120737466503)
XLA Ops:
  7.5 1.0 copy-done
  9.1 4.9 %all-to-all-start.1 = ((bf16[4,2,512]{2,1,0:T(2,128)(2,1)}), bf16[4,2,512]{2,1,0:T(2,128)(2,1)S(1)}, u32[]{:S(2)}, u32[]{:S(2)}) async-start(bf16[4,2,512]{2,1,0:T(2,128)(2,1)} %all_to_all.41), calls=%async_computation.2 | async-start | bytes 16384 | tf_op jit(solution)/shard_map/all_to_all | solution.py:125
  15.3 12.6 %pmax.7 = f32[8]{0:T(128)S(1)} all-reduce(f32[8]{0:T(128)S(1)} %get-tuple-element.49), channel_id=1, replica_groups=mesh['group'=8,'tp'=4] {'tp'}, use_global_device_ids=true, to_apply=%region_12.13 | all-reduce | flops 8 | bytes 64 | tf_op jit(solution)/shard_map/pmax | solution.py:136
  28.4 12.9 %reduce-scatter.2.cloned.1.call-done = bf16[64,2048]{1,0:T(8,128)(2,1)} async-done(((bf16[256,2048]{1,0:T(8,128)(2,1)}), bf16[64,2048]{1,0:T(8,128)(2,1)}) %reduce-scatter.2.cloned.1.call-update) | async-done | bytes 262160 | tf_op jit(solution)/shard_map/reduce_scatter | solution.py:101
  41.3 3.4 %collective-permute-start = (bf16[64,2048]{1,0:T(8,128)(2,1)}, bf16[64,2048]{1,0:T(8,128)(2,1)S(1)}, u32[]{:S(2)}, u32[]{:S(2)}) collective-permute-start(bf16[64,2048]{1,0:T(8,128)(2,1)} %reduce-scatter.2.cloned.1.call-done), channel_id=1, source_target_pairs={{0,8},{4,12},{8,16},{12,20},{16,24},{20,28},{1,9},{5,13},{9,17},{1... | collective-permute-start | bytes 786440 | tf_op jit(solution)/shard_map/ppermute | solution.py:19
  44.7 1.3 %collective-permute-start.1 = (bf16[64,2048]{1,0:T(8,128)(2,1)}, bf16[64,2048]{1,0:T(8,128)(2,1)S(1)}, u32[]{:S(2)}, u32[]{:S(2)}) collective-permute-start(bf16[64,2048]{1,0:T(8,128)(2,1)} %reduce-scatter.2.cloned.1.call-done), channel_id=1, source_target_pairs={{0,16},{4,20},{8,24},{12,28},{1,17},{5,21},{9,25},{13,29},{2,18},{... | collective-permute-start | bytes 786440 | tf_op jit(solution)/shard_map/ppermute | solution.py:19
  46.0 0.7 collective-permute-start.2
  46.9 5.2 %collective-permute-done = bf16[64,2048]{1,0:T(8,128)(2,1)S(1)} collective-permute-done((bf16[64,2048]{1,0:T(8,128)(2,1)}, bf16[64,2048]{1,0:T(8,128)(2,1)S(1)}, u32[]{:S(2)}, u32[]{:S(2)}) %collective-permute-start) | collective-permute-done | bytes 262176 | tf_op jit(solution)/shard_map/ppermute | solution.py:19
  52.1 5.5 %collective-permute-done.1 = bf16[64,2048]{1,0:T(8,128)(2,1)S(1)} collective-permute-done((bf16[64,2048]{1,0:T(8,128)(2,1)}, bf16[64,2048]{1,0:T(8,128)(2,1)S(1)}, u32[]{:S(2)}, u32[]{:S(2)}) %collective-permute-start.1) | collective-permute-done | bytes 262176 | tf_op jit(solution)/shard_map/ppermute | solution.py:19
  57.6 0.8 select_select_fusion
  58.4 9.2 %psum.7 = f32[8]{0:T(128)S(1)} all-reduce(f32[8]{0:T(128)S(1)} %fusion.4), channel_id=1, replica_groups=mesh['group'=8,'tp'=4] {'tp'}, use_global_device_ids=true, to_apply=%region_14.15 | all-reduce | flops 8 | bytes 64 | tf_op jit(solution)/shard_map/psum | solution.py:138
  68.4 0.7 fusion.21
  69.3 1.3 %copy.34 = bf16[2,128,2048]{1,2,0:T(8,128)(2,1)} copy(bf16[2,128,2048]{2,1,0:T(8,128)(2,1)S(1)} %copy-done.2) | data formatting | bytes 2097152 | tf_op args[4]
  71.2 3.3 %all-to-all-start = ((bf16[4,2,2048]{2,1,0:T(2,128)(2,1)}), bf16[4,2,2048]{2,1,0:T(2,128)(2,1)S(1)}, u32[]{:S(2)}, u32[]{:S(2)}) async-start(bf16[4,2,2048]{2,1,0:T(2,128)(2,1)} %all_to_all.38), calls=%async_computation.1 | async-start | bytes 65536 | tf_op jit(solution)/shard_map/all_to_all | solution.py:124
  74.5 6.0 %all-to-all-done = bf16[4,2,2048]{2,1,0:T(2,128)(2,1)S(1)} async-done(((bf16[4,2,2048]{2,1,0:T(2,128)(2,1)}), bf16[4,2,2048]{2,1,0:T(2,128)(2,1)S(1)}, u32[]{:S(2)}, u32[]{:S(2)}) %all-to-all-start) | async-done | bytes 32800 | tf_op jit(solution)/shard_map/all_to_all | solution.py:124
  80.7 6.0 %all-gather.2.cloned.1.call-done = bf16[256,2048]{1,0:T(8,128)(2,1)} async-done(((bf16[64,2048]{1,0:T(8,128)(2,1)}), bf16[256,2048]{1,0:T(8,128)(2,1)}) %all-gather.2.cloned.1.call-update) | async-done | bytes 1048592 | tf_op jit(solution)/shard_map/all_gather | solution.py:117
  86.6 1.4 %pad.5 = bf16[384,2048]{1,0:T(8,128)(2,1)S(1)} pad(bf16[256,2048]{1,0:T(8,128)(2,1)} %all-gather.2.cloned.1.call-done, bf16[]{:T(256)} %constant.55.clone.1), padding=0_128x0_0 | pad | bytes 2621442 | tf_op jit(solution)/shard_map/jit(_pad)/pad | solution.py:118
  88.0 2.7 %while.1 = (s32[]{:T(128)}, bf16[384,2048]{1,0:T(8,128)(2,1)S(1)}, s32[2,2]{1,0:T(2,128)S(1)}, bf16[2,128,2048]{1,2,0:T(8,128)(2,1)}, s32[]{:T(128)}) while((s32[]{:T(128)}, bf16[384,2048]{1,0:T(8,128)(2,1)S(1)}, s32[2,2]{1,0:T(2,128)S(1)}, bf16[2,128,2048]{1,2,0:T(8,128)(2,1)}, s32[]{:T(128)}) %tuple.40), condition=%wide.while_cond, body=%wide.while_body.sunk | while | flops 2 | bytes 3146325 | solution.py:119
  88.5 0.9 constant_dynamic-update-slice_fusion.2
  89.8 0.9 constant_dynamic-update-slice_fusion.2
  90.7 1.7 %broadcast_select_fusion = bf16[2,128,2048]{1,2,0:T(8,128)(2,1)S(1)} fusion(bf16[2,128,2048]{1,2,0:T(8,128)(2,1)} %get-tuple-element.22, bf16[2,128,2048]{1,2,0:T(8,128)(2,1)} %copy.34, pred[2]{0:T(512)(128)(4,1)S(1)} %get-tuple-element.52), kind=kLoop, calls=%fused_computation.6 | loop fusion | flops 524288 | bytes 3145730 | tf_op jit(solution)/shard_map/jit(_where)/select_n | solution.py:120
  94.1 3.3 %all-to-all-start.2 = ((bf16[2,4,2048]{2,0,1:T(2,128)(2,1)}), bf16[2,4,2048]{2,0,1:T(2,128)(2,1)S(1)}, u32[]{:S(2)}, u32[]{:S(2)}) async-start(bf16[2,4,2048]{2,0,1:T(2,128)(2,1)} %copy.38), calls=%async_computation.3 | async-start | bytes 65536 | tf_op jit(solution)/shard_map/all_to_all | solution.py:128
  97.4 0.8 fusion.5
  98.2 4.8 %all-to-all-done.2 = bf16[2,4,2048]{2,0,1:T(2,128)(2,1)S(1)} async-done(((bf16[2,4,2048]{2,0,1:T(2,128)(2,1)}), bf16[2,4,2048]{2,0,1:T(2,128)(2,1)S(1)}, u32[]{:S(2)}, u32[]{:S(2)}) %all-to-all-start.2) | async-done | bytes 32800 | tf_op jit(solution)/shard_map/all_to_all | solution.py:128
  (74 shorter events, 8.1 us)
Async XLA Ops:
  7.2 34.2 %reduce-scatter.2.cloned.1.call-start = ((), (), s32[]{:S(2)}) async-start(), calls=%async_computation.4 | async-start | bytes 1310720 | tf_op jit(solution)/shard_map/reduce_scatter | solution.py:101
  7.2 1.2 %copy-start.5 = (bf16[8,512]{1,0:T(8,128)(2,1)S(1)}, bf16[8,512]{1,0:T(8,128)(2,1)}, u32[]{:S(2)}) copy-start(bf16[8,512]{1,0:T(8,128)(2,1)} %param.20) | copy-start | bytes 24580
  7.2 6.7 %copy-start.9 = (s32[8]{0:T(128)S(1)}, s32[8]{0:T(128)}, u32[]{:S(2)}) copy-start(s32[8]{0:T(128)} %param.22) | copy-start | bytes 100
  7.2 6.8 %copy-start.4 = (s32[24,256]{1,0:T(8,128)S(1)}, s32[24,256]{1,0:T(8,128)}, u32[]{:S(2)}) copy-start(s32[24,256]{1,0:T(8,128)} %param.23) | copy-start | bytes 73732
  7.3 7.9 %copy-start.1 = (bf16[8,7680]{1,0:T(8,128)(2,1)S(1)}, bf16[8,7680]{1,0:T(8,128)(2,1)}, u32[]{:S(2)}) copy-start(bf16[8,7680]{1,0:T(8,128)(2,1)} %param.21) | copy-start | bytes 368644
  7.3 20.7 %copy-start.8 = (s32[2,8]{1,0:T(2,128)S(1)}, s32[2,8]{1,0:T(2,128)}, u32[]{:S(2)}) copy-start(s32[2,8]{1,0:T(2,128)} %param.15) | copy-start | bytes 196
  7.3 39.4 %copy-start.6 = (s32[2,8]{1,0:T(2,128)S(1)}, s32[2,8]{1,0:T(2,128)}, u32[]{:S(2)}) copy-start(s32[2,8]{1,0:T(2,128)} %param.16) | copy-start | bytes 196
  7.3 61.1 %copy-start.7 = (s32[2]{0:T(128)S(1)}, s32[2]{0:T(128)}, u32[]{:S(2)}) copy-start(s32[2]{0:T(128)} %param.18) | copy-start | bytes 28
  7.3 62.0 %copy-start.2 = (bf16[2,128,2048]{2,1,0:T(8,128)(2,1)S(1)}, bf16[2,128,2048]{2,1,0:T(8,128)(2,1)}, u32[]{:S(2)}) copy-start(bf16[2,128,2048]{2,1,0:T(8,128)(2,1)} %param.17) | copy-start | bytes 3145732
  7.3 63.3 %copy-start.3 = (bf16[8,2048]{1,0:T(8,128)(2,1)S(1)}, bf16[8,2048]{1,0:T(8,128)(2,1)}, u32[]{:S(2)}) copy-start(bf16[8,2048]{1,0:T(8,128)(2,1)} %param.19) | copy-start | bytes 98308
  7.4 1.0 copy-start
  9.1 62.1 %all-to-all-start.1 = ((bf16[4,2,512]{2,1,0:T(2,128)(2,1)}), bf16[4,2,512]{2,1,0:T(2,128)(2,1)S(1)}, u32[]{:S(2)}, u32[]{:S(2)}) async-start(bf16[4,2,512]{2,1,0:T(2,128)(2,1)} %all_to_all.41), calls=%async_computation.2 | async-start | bytes 16384 | tf_op jit(solution)/shard_map/all_to_all | solution.py:125
  14.0 72.7 %all-gather.2.cloned.1.call-start = ((), (), s32[]{:S(2)}) async-start(), calls=%async_computation.5 | async-start | bytes 1310720 | tf_op jit(solution)/shard_map/all_gather | solution.py:117
  41.3 10.7 %collective-permute-start = (bf16[64,2048]{1,0:T(8,128)(2,1)}, bf16[64,2048]{1,0:T(8,128)(2,1)S(1)}, u32[]{:S(2)}, u32[]{:S(2)}) collective-permute-start(bf16[64,2048]{1,0:T(8,128)(2,1)} %reduce-scatter.2.cloned.1.call-done), channel_id=1, source_target_pairs={{0,8},{4,12},{8,16},{12,20},{16,24},{20,28},{1,9},{5,13},{9,17},{1... | collective-permute-start | bytes 786440 | tf_op jit(solution)/shard_map/ppermute | solution.py:19
  44.7 12.9 %collective-permute-start.1 = (bf16[64,2048]{1,0:T(8,128)(2,1)}, bf16[64,2048]{1,0:T(8,128)(2,1)S(1)}, u32[]{:S(2)}, u32[]{:S(2)}) collective-permute-start(bf16[64,2048]{1,0:T(8,128)(2,1)} %reduce-scatter.2.cloned.1.call-done), channel_id=1, source_target_pairs={{0,16},{4,20},{8,24},{12,28},{1,17},{5,21},{9,25},{13,29},{2,18},{... | collective-permute-start | bytes 786440 | tf_op jit(solution)/shard_map/ppermute | solution.py:19
  46.0 11.6 %collective-permute-start.2 = (bf16[64,2048]{1,0:T(8,128)(2,1)}, bf16[64,2048]{1,0:T(8,128)(2,1)S(1)}, u32[]{:S(2)}, u32[]{:S(2)}) collective-permute-start(bf16[64,2048]{1,0:T(8,128)(2,1)} %reduce-scatter.2.cloned.1.call-done), channel_id=1, source_target_pairs={{0,24},{4,28},{1,25},{5,29},{2,26},{6,30},{3,27},{7,31}} | collective-permute-start | bytes 786440 | tf_op jit(solution)/shard_map/ppermute | solution.py:19
  71.2 9.3 %all-to-all-start = ((bf16[4,2,2048]{2,1,0:T(2,128)(2,1)}), bf16[4,2,2048]{2,1,0:T(2,128)(2,1)S(1)}, u32[]{:S(2)}, u32[]{:S(2)}) async-start(bf16[4,2,2048]{2,1,0:T(2,128)(2,1)} %all_to_all.38), calls=%async_computation.1 | async-start | bytes 65536 | tf_op jit(solution)/shard_map/all_to_all | solution.py:124
  94.1 8.9 %all-to-all-start.2 = ((bf16[2,4,2048]{2,0,1:T(2,128)(2,1)}), bf16[2,4,2048]{2,0,1:T(2,128)(2,1)S(1)}, u32[]{:S(2)}, u32[]{:S(2)}) async-start(bf16[2,4,2048]{2,0,1:T(2,128)(2,1)} %copy.38), calls=%async_computation.3 | async-start | bytes 65536 | tf_op jit(solution)/shard_map/all_to_all | solution.py:128
Sparse Core Ops, SparseCore 0:
  10.3 31.0 reduce-scatter.1
  58.5 28.0 all-gather.1
where the time goes:
time: 113 us; the launch traced here: 110 us
  waiting for transfers between devices  40.4 us (36%)
  blocking collectives  21.8 us (19%)
  starting transfers between devices  16.8 us (15%)
  between operations  14.3 us (13%)
  local copies, waits for them, and re-layouts  10.2 us (9%)
  other arithmetic  6.08 us (5%)
    reduce_scatter x1, waiting for transfers between devices, per_device(): lax.psum_scatter(lax.cond(is_prefill, compute, lambda: jnp.zeros((token_c...  12.9 us
    pmax x1, blocking collectives, per_device(): highest = lax.pmax(local_peak, 'tp')  12.6 us
    ppermute x3, waiting for transfers between devices, from_behind(): return lax.ppermute(block, axis, route)  10.7 us
    psum x1, blocking collectives, per_device(): denominator = lax.psum(local_terms, 'tp')  9.17 us
    all_gather x1, waiting for transfers between devices, per_device(): gathered = lax.all_gather(incoming, 'tp', axis=0, tiled=True)  5.97 us
    all_to_all x1, waiting for transfers between devices, per_device(): lax.all_to_all(queries, 'tp', split_axis=0, concat_axis=1, tiled=True)  5.96 us
    ppermute x3, starting transfers between devices, from_behind(): return lax.ppermute(block, axis, route)  5.33 us
    all_to_all x1, starting transfers between devices, per_device(): lax.all_to_all(fresh, 'tp', split_axis=0, concat_axis=1, tiled=True)  4.87 us
  transfers between devices with their start and end apart: 8, of which 6 were waited for; matrix products, arithmetic and copies ran while one was open for 6% of the time, Pallas kernels for 0%

commit v1 on v0

v1 whole, which is shorter than its diff:
```python
import functools
import math

import jax
import jax.numpy as jnp
from jax import lax
from jax.experimental import pallas as pl
from jax.experimental.pallas import tpu as pltpu
from jax.sharding import PartitionSpec as P

HEADS = 64
KVH = 8
HD = 128
GQ = HEADS // KVH
TURNS = 4
BITS = 30
MESH = pl.DeviceIdType.MESH
F32 = jnp.float32
BF16 = jnp.bfloat16


def segments(block):
    u = block // 8
    return (
        (0, 0, 2 * u, 0),
        (0, 2 * u, 2 * u, 2 * u),
        (1, 4 * u, u, 0),
        (2, 5 * u, 2 * u, 0),
        (3, 7 * u, u, 0),
    )


def kernel(
    n, groups,
    plen, ostep, clen, states, hidden, w_kv, cache, queries, fresh, logits, masks,
    att_out, lp_out,
    hid, w, part, rsbuf, kv, cv, qv, frv, lgv, mkv, packed, qs, qrecv, osend, orecv,
    frall, stat, lp, att,
    lsem, wsem, hsend, hrecv, rssend, rsrecv, agsend, agrecv,
    qsend, qrsem, fsend, frsem, osem, orsem, ssend, srsem,
):
    g = lax.axis_index("group")
    c = lax.axis_index("tp")
    prefill = groups // TURNS
    p = lax.rem(g, prefill)
    turn = g // prefill
    block, dl = hidden.shape
    rows, vdev = logits.shape
    own = cache.shape[0]
    npos = cache.shape[1]
    hq = HEADS // n
    gq = min(GQ, hq)
    kh = max(1, hq // GQ)
    kw = kh * HD
    oh = own * hq
    fw = fresh.shape[1]
    half = KVH * HD
    segs = segments(block)
    scale = 1.0 / math.sqrt(HD)

    def peer(o):
        return lax.rem(c + o, n)

    def kv_first(d):
        return (d * hq) // GQ

    barrier = pltpu.get_barrier_semaphore()

    def hello(o, carry):
        pl.semaphore_signal(barrier, inc=1, device_id=(g, peer(o)), device_id_type=MESH)
        return carry

    lax.fori_loop(1, n, hello, 0)
    for o in range(1, TURNS):
        pl.semaphore_signal(
            barrier, inc=1, device_id=(lax.rem(g + o * prefill, groups), c), device_id_type=MESH
        )

    small = [
        pltpu.make_async_copy(src, dst, lsem.at[i])
        for i, (src, dst) in enumerate(
            ((queries, qv), (fresh, frv), (logits, lgv), (cache, cv))
        )
    ]
    small += [
        pltpu.make_async_copy(masks.at[:, k * HD : (k + 1) * HD], mkv.at[k], lsem.at[6 + k])
        for k in range(mkv.shape[0])
    ]
    own_tokens = part.shape[1]
    own_hidden = pltpu.make_async_copy(hidden.at[pl.ds(0, own_tokens)], hid, lsem.at[5])

    def w_copies(d):
        first = pl.multiple_of(kv_first(d) * HD, HD)
        return [
            pltpu.make_async_copy(
                w_kv.at[:, pl.ds(pl.multiple_of(first + s * half, HD), kw)],
                w.at[d, :, pl.ds(s * kw, kw)],
                wsem.at[d, s],
            )
            for s in range(2)
        ]

    small[0].start()
    small[1].start()

    @pl.when(turn == 0)
    def _():
        own_hidden.start()

    def start_w(o, carry):
        for copy in w_copies(peer(o)):
            copy.start()
        return carry

    lax.fori_loop(1, n, start_w, 0)
    for copy in small[2:]:
        copy.start()
    start_w(0, 0)

    pl.semaphore_wait(barrier, n - 1 + TURNS - 1)

    def spread(t, start, size, loff):
        return pltpu.make_async_remote_copy(
            src_ref=hidden.at[pl.ds(start, size)],
            dst_ref=hid.at[pl.ds(loff, size)],
            send_sem=hsend.at[t],
            recv_sem=hrecv,
            device_id=(p + t * prefill, c),
            device_id_type=MESH,
        )

    @pl.when(turn == 0)
    def _():
        for t, start, size, loff in segs:
            if t > 0:
                spread(t, start, size, loff).start()

    small[0].wait()
    small[1].wait()
    for h in range(hq):
        qs[pl.ds(h, rows, stride=hq), :] = qv[:, h * HD : (h + 1) * HD].astype(F32)
    for k in range(fw // HD):
        frall[pl.ds(c, 1), k] = frv[:, k * HD : (k + 1) * HD].astype(F32)[None]

    def q_copy(d, slot):
        return pltpu.make_async_remote_copy(
            src_ref=qs.at[pl.ds(pl.multiple_of(d * oh, oh), oh)],
            dst_ref=qrecv.at[slot],
            send_sem=qsend.at[d],
            recv_sem=qrsem.at[slot],
            device_id=(g, d),
            device_id_type=MESH,
        )

    def f_copy(d, slot):
        return pltpu.make_async_remote_copy(
            src_ref=frall.at[c],
            dst_ref=frall.at[slot],
            send_sem=fsend.at[d],
            recv_sem=frsem.at[slot],
            device_id=(g, d),
            device_id_type=MESH,
        )

    def send_q(o, carry):
        q_copy(peer(o), c).start()
        f_copy(peer(o), c).start()
        return carry

    lax.fori_loop(1, n, send_q, 0)
    qrecv[pl.ds(c, 1)] = qs[pl.ds(pl.multiple_of(c * oh, oh), oh), :][None]

    def rs_copy(s, d, slot):
        _, _, size, loff = segs[s]
        return pltpu.make_async_remote_copy(
            src_ref=part.at[d, pl.ds(loff, size)],
            dst_ref=rsbuf.at[slot, pl.ds(loff, size)],
            send_sem=rssend.at[s, d],
            recv_sem=rsrecv.at[s, slot],
            device_id=(g, d),
            device_id_type=MESH,
        )

    def project(s, wait_w):
        _, _, size, loff = segs[s]

        def one(o, carry):
            d = peer(o)
            if wait_w:
                for copy in w_copies(d):
                    copy.wait()
            part[d, pl.ds(loff, size), :] = jnp.dot(
                hid[pl.ds(loff, size), :], w[d], preferred_element_type=F32
            ).astype(BF16)
            rs_copy(s, d, c).start()
            return carry

        lax.fori_loop(1, n, one, 0)

    def own_part(s, wait_w):
        _, _, size, loff = segs[s]
        if wait_w:
            for copy in w_copies(c):
                copy.wait()
        return jnp.dot(hid[pl.ds(loff, size), :], w[c], preferred_element_type=F32)

    def ag_copy(s, t):
        _, start, size, _ = segs[s]
        ref = kv.at[pl.ds(start, size)]
        return pltpu.make_async_remote_copy(
            src_ref=ref,
            dst_ref=ref,
            send_sem=agsend.at[s, t],
            recv_sem=agrecv.at[s],
            device_id=(p + t * prefill, c),
            device_id_type=MESH,
        )

    def finish(s, wait_w):
        owner, start, size, loff = segs[s]
        total = own_part(s, wait_w)
        for o in range(1, n):
            src = peer(n - o)
            rs_copy(s, src, src).wait_recv()
            total = total + rsbuf[src, pl.ds(loff, size), :].astype(F32)
        kv[pl.ds(start, size), :] = total.astype(BF16)
        for t in range(1, TURNS):
            if t != owner:
                ag_copy(s, t).start()

    @pl.when(turn == 0)
    def _():
        own_hidden.wait()
        project(0, True)
        project(1, False)

    small[2].wait()
    for copy in small[4:]:
        copy.wait()
    for r in range(rows):
        for k in range(mkv.shape[0]):
            packed[k, pl.ds(r, 1), :] = mkv[k, pl.ds(states[r], 1), :]
    words = HD
    span = words * BITS
    token = lax.broadcasted_iota(jnp.int32, (words, span), 1)
    gap = token - BITS * lax.broadcasted_iota(jnp.int32, (words, span), 0)
    expand = jnp.where((gap >= 0) & (gap < BITS), 1.0, 0.0).astype(BF16)
    lane = lax.broadcasted_iota(jnp.int32, (rows, span), 1)
    lane_f = lane.astype(F32)
    bit = lane - BITS * jnp.floor((lane_f + 0.5) / BITS).astype(jnp.int32)
    shift = jnp.bitwise_and(bit, 7)
    peak = jnp.full((rows, 1), -jnp.inf, F32)
    for k in range(vdev // span):
        word = packed[k]
        pieces = jnp.concatenate(
            [
                jnp.bitwise_and(jnp.right_shift(word, 8 * i), 255).astype(F32)
                for i in range(4)
            ],
            axis=0,
        ).astype(BF16)
        got = jnp.dot(pieces, expand, preferred_element_type=F32)
        low = jnp.where(bit < 8, got[:rows], got[rows : 2 * rows])
        high = jnp.where(bit < 24, got[2 * rows : 3 * rows], got[3 * rows :])
        byte = jnp.where(bit < 16, low, high).astype(jnp.int32)
        ok = jnp.bitwise_and(jnp.right_shift(byte, shift), 1) == 1
        value = jnp.where(ok, lgv[:, k * span : (k + 1) * span].astype(F32), -jnp.inf)
        lp[:, k * span : (k + 1) * span] = value
        peak = jnp.maximum(peak, jnp.max(value, axis=1, keepdims=True))
    terms = jnp.sum(jnp.exp(lp[...] - peak), axis=1, keepdims=True)
    stat[pl.ds(c, 1), 0] = jnp.broadcast_to(peak, (rows, HD))[None]
    stat[pl.ds(c, 1), 1] = jnp.broadcast_to(terms, (rows, HD))[None]

    def s_copy(d, slot):
        return pltpu.make_async_remote_copy(
            src_ref=stat.at[c],
            dst_ref=stat.at[slot],
            send_sem=ssend.at[d],
            recv_sem=srsem.at[slot],
            device_id=(g, d),
            device_id_type=MESH,
        )

    def send_s(o, carry):
        s_copy(peer(o), c).start()
        return carry

    lax.fori_loop(1, n, send_s, 0)

    def recv_q(o, carry):
        src = peer(o)
        q_copy(src, src).wait_recv()
        f_copy(src, src).wait_recv()
        return carry

    lax.fori_loop(1, n, recv_q, 0)
    small[3].wait()
    position = lax.broadcasted_iota(jnp.int32, (1, npos), 1)

    def own_rows(i, first):
        out = []
        for h in range(KVH):
            col = first + h * HD
            row = frall[col // fw, col % fw // HD, pl.ds(c * own + i, 1), :]
            out.append(jnp.broadcast_to(row, (GQ, HD)))
        return jnp.concatenate(out, axis=0)

    for i in range(own):
        query = jnp.concatenate([qrecv[d, i * hq : (i + 1) * hq, :] for d in range(n)], axis=0)
        score = jnp.concatenate(
            [
                lax.dot_general(
                    query[h * GQ : (h + 1) * GQ].astype(BF16),
                    cv[i, :, h * HD : (h + 1) * HD],
                    (((1,), (1,)), ((), ())),
                    preferred_element_type=F32,
                )
                for h in range(KVH)
            ],
            axis=0,
        )
        score = jnp.where(position < clen[i], score * scale, -jnp.inf)
        mine = jnp.sum(query * own_rows(i, 0), axis=1, keepdims=True) * scale
        top = jnp.maximum(jnp.max(score, axis=1, keepdims=True), mine)
        expo = jnp.exp(score - top)
        mine = jnp.exp(mine - top)
        denom = jnp.sum(expo, axis=1, keepdims=True) + mine
        weight = expo / denom
        mine = (mine / denom).astype(BF16).astype(F32)
        result = jnp.concatenate(
            [
                jnp.dot(
                    weight[h * GQ : (h + 1) * GQ].astype(BF16),
                    cv[i, :, half + h * HD : half + (h + 1) * HD],
                    preferred_element_type=F32,
                )
                for h in range(KVH)
            ],
            axis=0,
        )
        result = result + mine * own_rows(i, half)
        for d in range(n):
            osend[d, i * hq : (i + 1) * hq, :] = result[d * hq : (d + 1) * hq]

    def o_copy(d, slot):
        return pltpu.make_async_remote_copy(
            src_ref=osend.at[d],
            dst_ref=orecv.at[pl.ds(pl.multiple_of(slot * oh, oh), oh)],
            send_sem=osem.at[d],
            recv_sem=orsem.at[slot],
            device_id=(g, d),
            device_id_type=MESH,
        )

    def send_o(o, carry):
        o_copy(peer(o), c).start()
        return carry

    lax.fori_loop(1, n, send_o, 0)
    orecv[pl.ds(pl.multiple_of(c * oh, oh), oh), :] = osend[c]

    for s, (owner, start, size, loff) in enumerate(segs):
        if owner > 0:

            @pl.when(turn == owner)
            def _(s=s, owner=owner, start=start, size=size, loff=loff):
                spread(owner, start, size, loff).wait_recv()
                project(s, True)

    @pl.when(turn == 0)
    def _():
        finish(0, True)
        finish(1, False)

    def recv_s(o, carry):
        src = peer(o)
        s_copy(src, src).wait_recv()
        return carry

    lax.fori_loop(1, n, recv_s, 0)
    peaks = stat[0, 0]
    for d in range(1, n):
        peaks = jnp.maximum(peaks, stat[d, 0])
    total = jnp.zeros_like(peaks)
    for d in range(n):
        total = total + stat[d, 1] * jnp.exp(stat[d, 0] - peaks)
    norm = (peaks + jnp.log(total))[:, :1]
    value = lp[...]
    lp[...] = jnp.where(value == -jnp.inf, 0.0, value - norm)
    lp_copy = pltpu.make_async_copy(lp, lp_out, lsem.at[2])
    lp_copy.start()

    line = lax.broadcasted_iota(jnp.int32, (rows, 1), 0)
    slot = lax.rem(line, own) * n + line // own
    spot = lax.broadcasted_iota(jnp.int32, (rows, block), 1)
    begin = jnp.full((rows, 1), 0, jnp.int32)
    length = jnp.full((rows, 1), 0, jnp.int32)
    at = jnp.int32(0)
    rank = jnp.int32(0)
    for k in range(plen.shape[1]):
        size = plen[p, k]
        chosen = (ostep[p, k] == turn).astype(jnp.int32)
        hit = slot == rank * chosen - (1 - chosen)
        begin = jnp.where(hit, at, begin)
        length = jnp.where(hit, size, length)
        at = at + size
        rank = rank + chosen
    landed = length > 0
    bias = jnp.where((spot >= begin) & (spot < begin + length), 0.0, -jnp.inf)

    for s, (owner, start, size, loff) in enumerate(segs):
        if owner > 0:

            @pl.when(turn == owner)
            def _(s=s):
                finish(s, True)

    def recv_o(o, carry):
        src = peer(o)
        o_copy(src, src).wait_recv()
        return carry

    lax.fori_loop(1, n, recv_o, 0)

    @pl.when(turn == 0)
    def _():
        for h in range(hq):
            att[:, h * HD : (h + 1) * HD] = orecv[pl.ds(h, rows, stride=hq), :].astype(BF16)

    @pl.when(turn > 0)
    def _():
        for s, (owner, start, size, loff) in enumerate(segs):

            @pl.when(turn != owner)
            def _(s=s):
                ag_copy(s, 0).wait_recv()

        biases = jnp.concatenate([bias] * gq, axis=0)
        for j in range(kh):
            query = jnp.concatenate(
                [
                    qv[:, (j * gq + x) * HD : (j * gq + x + 1) * HD].astype(F32)
                    for x in range(gq)
                ],
                axis=0,
            )

            def mine_of(first):
                col = first + (kv_first(c) + j) * HD
                return jnp.concatenate([frall[col // fw, lax.rem(col, fw) // HD]] * gq, axis=0)

            score = lax.dot_general(
                query.astype(BF16),
                kv[:, j * HD : (j + 1) * HD],
                (((1,), (1,)), ((), ())),
                preferred_element_type=F32,
            )
            score = score * scale + biases
            mine = jnp.sum(query * mine_of(0), axis=1, keepdims=True) * scale
            top = jnp.maximum(jnp.max(score, axis=1, keepdims=True), mine)
            expo = jnp.exp(score - top)
            mine = jnp.exp(mine - top)
            denom = jnp.sum(expo, axis=1, keepdims=True) + mine
            weight = (expo / denom).astype(BF16)
            mine = (mine / denom).astype(BF16).astype(F32)
            result = jnp.dot(
                weight, kv[:, kw + j * HD : kw + (j + 1) * HD], preferred_element_type=F32
            )
            result = result + mine * mine_of(half)
            for x in range(gq):
                h = j * gq + x
                cached = orecv[pl.ds(h, rows, stride=hq), :]
                att[:, h * HD : (h + 1) * HD] = jnp.where(
                    landed, result[x * rows : (x + 1) * rows], cached
                ).astype(BF16)

    att_copy = pltpu.make_async_copy(att, att_out, lsem.at[0])
    att_copy.start()

    def drain(o, carry):
        d = peer(o)
        q_copy(d, c).wait_send()
        f_copy(d, c).wait_send()
        s_copy(d, c).wait_send()
        o_copy(d, c).wait_send()
        return carry

    lax.fori_loop(1, n, drain, 0)

    for s, (owner, start, size, loff) in enumerate(segs):

        @pl.when(turn == owner)
        def _(s=s, owner=owner):
            def drain_rs(o, carry):
                rs_copy(s, peer(o), c).wait_send()
                return carry

            lax.fori_loop(1, n, drain_rs, 0)
            for t in range(1, TURNS):
                if t != owner:
                    ag_copy(s, t).wait_send()

    @pl.when(turn == 0)
    def _():
        for t, start, size, loff in segs:
            if t > 0:
                spread(t, start, size, loff).wait_send()

    lp_copy.wait()
    att_copy.wait()


def solution(mesh):
    n = mesh.shape["tp"]
    groups = mesh.shape["group"]

    def per_device(
        hidden, w_kv, plen, ostep, cache, clen, queries, fresh, logits, states, masks
    ):
        block, dl = hidden.shape
        rows, vdev = logits.shape
        own, npos, kvw = cache.shape
        hq = HEADS // n
        kw2 = 2 * max(1, hq // GQ) * HD
        oh = own * hq
        fw = fresh.shape[1]
        segs = segments(block)
        ns = len(segs)
        tmax = max(size + loff for _, _, size, loff in segs)
        dma = pltpu.SemaphoreType.DMA
        smem = pl.BlockSpec(memory_space=pltpu.SMEM)
        anys = pl.BlockSpec(memory_space=pl.ANY)
        return pl.pallas_call(
            functools.partial(kernel, n, groups),
            out_shape=(
                jax.ShapeDtypeStruct(queries.shape, BF16),
                jax.ShapeDtypeStruct(logits.shape, F32),
            ),
            in_specs=[smem] * 4 + [anys] * 7,
            out_specs=(anys, anys),
            scratch_shapes=[
                pltpu.VMEM((tmax, dl), BF16),
                pltpu.VMEM((n, dl, kw2), BF16),
                pltpu.VMEM((n, tmax, kw2), BF16),
                pltpu.VMEM((n, tmax, kw2), BF16),
                pltpu.VMEM((block, kw2), BF16),
                pltpu.VMEM(cache.shape, BF16),
                pltpu.VMEM(queries.shape, BF16),
                pltpu.VMEM(fresh.shape, BF16),
                pltpu.VMEM(logits.shape, BF16),
                pltpu.VMEM((masks.shape[1] // HD,) + (masks.shape[0], HD), jnp.int32),
                pltpu.VMEM((masks.shape[1] // HD, rows, HD), jnp.int32),
                pltpu.VMEM((rows * hq, HD), F32),
                pltpu.VMEM((n, oh, HD), F32),
                pltpu.VMEM((n, oh, HD), F32),
                pltpu.VMEM((rows * hq, HD), F32),
                pltpu.VMEM((n, fw // HD, rows, HD), F32),
                pltpu.VMEM((n, 2, rows, HD), F32),
                pltpu.VMEM(logits.shape, F32),
                pltpu.VMEM(queries.shape, BF16),
                dma((6 + masks.shape[1] // HD,)),
                dma((n, 2)),
                dma((TURNS,)),
                dma,
                dma((ns, n)),
                dma((ns, n)),
                dma((ns, TURNS)),
                dma((ns,)),
                dma((n,)),
                dma((n,)),
                dma((n,)),
                dma((n,)),
                dma((n,)),
                dma((n,)),
                dma((n,)),
                dma((n,)),
            ],
            compiler_params=pltpu.CompilerParams(
                collective_id=0, has_side_effects=True, vmem_limit_bytes=60 * 1024 * 1024
            ),
        )(plen, ostep, clen, states, hidden, w_kv, cache, queries, fresh, logits, masks)

    in_specs = (
        P("group", "tp"),
        P("tp", None),
        P(),
        P(),
        P(("group", "tp"), None, None),
        P(("group", "tp")),
        P("group", "tp"),
        P("group", "tp"),
        P("group", "tp"),
        P("group"),
        P(None, "tp"),
    )
    out_specs = (P("group", "tp"), P("group", "tp"))
    return jax.shard_map(
        per_device, mesh=mesh, in_specs=in_specs, out_specs=out_specs, check_vma=False
    )
```

time: 113 us -> 31.1 us (0.28)
  the two profiles are of different devices: /device:TPU:4 before, /device:TPU:14 now
where the time goes in v1:
time: 31.1 us; the launch traced here: 30.9 us
  Pallas kernels  27.2 us (87%)
  local copies, waits for them, and re-layouts  3.03 us (10%)
  between operations  0.64 us (2%)
    pallas_call x1, Pallas kernels, per_device(): pl.pallas_call(functools.partial(kernel, n, groups), out_shape=(jax.Shape...  27.2 us
    unnamed x2, local copies, waits for them, and re-layouts  3.03 us

profile of v1, /device:TPU:14, one launch (start us, length us, event | category | flops | bytes accessed | tf_op | source)
XLA Modules:
  0.0 30.9 jit_solution(11707502760238937921)
XLA Ops:
  0.6 27.2 %shard_map.122 = (bf16[8,2048]{1,0:T(8,128)(2,1)}, f32[8,7680]{1,0:T(8,128)}) custom-call(s32[2,8]{1,0:T(2,128)} %plen.1, s32[2,8]{1,0:T(2,128)} %ostep.1, s32[2]{0:T(128)} %clen.1, s32[8]{0:T(128)} %states.1, bf16[256,2048]{1,0:T(8,128)(2,1)} %hidden.1, bf16[2048,2048]{1,0:T(8,128)(2,1)} %w_kv.1, bf16[2,128,2048]{2,1,0:T(8,128)(2,1)} %cache.1, ...), custom_call_target="tpu_custom_call" | custom-call | tf_op jit(solution)/shard_map/pallas_call | solution.py:533
  27.9 1.4 %copy.15 = bf16[8,2048]{1,0:T(8,128)(2,1)} copy(bf16[8,2048]{1,0:T(8,128)(2,1)} %get-tuple-element.4) | data formatting | bytes 65536
  29.2 1.7 %copy.16 = f32[8,7680]{1,0:T(8,128)} copy(f32[8,7680]{1,0:T(8,128)} %get-tuple-element.5) | data formatting | bytes 491520

commit v2 on v1

--- a/solution.py
+++ b/solution.py
@@ -14,30 +14,31 @@
 GQ = HEADS // KVH
 TURNS = 4
 BITS = 30
+PLAN = ((0, 3), (0, 3), (1, 2), (2, 2), (3, 2), (2, 2), (1, 1), (3, 1))
 MESH = pl.DeviceIdType.MESH
 F32 = jnp.float32
 BF16 = jnp.bfloat16
 
 
 def segments(block):
-    u = block // 8
-    return (
-        (0, 0, 2 * u, 0),
-        (0, 2 * u, 2 * u, 2 * u),
-        (1, 4 * u, u, 0),
-        (2, 5 * u, 2 * u, 0),
-        (3, 7 * u, u, 0),
-    )
+    out, filled, at = [], [0] * TURNS, 0
+    for owner, share in PLAN:
+        size = block * share // 16
+        out.append((owner, at, size, filled[owner]))
+        filled[owner] += size
+        at += size
+    return tuple(out)
 
 
 def kernel(
     n, groups,
-    plen, ostep, clen, states, hidden, w_kv, cache, queries, fresh, logits, masks,
-    att_out, lp_out,
-    hid, w, part, rsbuf, kv, cv, qv, frv, lgv, mkv, packed, qs, qrecv, osend, orecv,
-    frall, stat, lp, att,
+    plen_in, ostep_in, clen_in, states_in, hidden, w_kv, cache, queries, fresh, logits, masks,
+    att, lp,
+    plen, ostep, clen, states,
+    hid, w, part, rsbuf, kv, cv, qv, fb, lgv, mkv, packed, qs, qb, qrecv, osend, orecv, of,
+    frall, stat,
     lsem, wsem, hsend, hrecv, rssend, rsrecv, agsend, agrecv,
-    qsend, qrsem, fsend, frsem, osem, orsem, ssend, srsem,
+    csem, qsend, qrsem, fsend, frsem, osem, orsem, ssend, srsem,
 ):
     g = lax.axis_index("group")
     c = lax.axis_index("tp")
@@ -79,15 +80,23 @@
     small = [
         pltpu.make_async_copy(src, dst, lsem.at[i])
         for i, (src, dst) in enumerate(
-            ((queries, qv), (fresh, frv), (logits, lgv), (cache, cv))
+            ((queries, qv), (fresh, fb.at[c]), (logits, lgv), (cache, cv))
         )
     ]
     small += [
         pltpu.make_async_copy(masks.at[:, k * HD : (k + 1) * HD], mkv.at[k], lsem.at[6 + k])
         for k in range(mkv.shape[0])
     ]
-    own_tokens = part.shape[1]
-    own_hidden = pltpu.make_async_copy(hidden.at[pl.ds(0, own_tokens)], hid, lsem.at[5])
+    scalars = [
+        pltpu.make_async_copy(src, dst, csem.at[i])
+        for i, (src, dst) in enumerate(
+            ((plen_in, plen), (ostep_in, ostep), (clen_in, clen), (states_in, states))
+        )
+    ]
+    own_tokens = sum(size for owner, _, size, _ in segs if owner == 0)
+    own_hidden = pltpu.make_async_copy(
+        hidden.at[pl.ds(0, own_tokens)], hid.at[pl.ds(0, own_tokens)], lsem.at[5]
+    )
 
     def w_copies(d):
         first = pl.multiple_of(kv_first(d) * HD, HD)
@@ -102,6 +111,8 @@
 
     small[0].start()
     small[1].start()
+    for copy in scalars:
+        copy.start()
 
     @pl.when(turn == 0)
     def _():
@@ -117,34 +128,33 @@
         copy.start()
     start_w(0, 0)
 
+    small[0].wait()
+    for h in range(hq):
+        qs[pl.ds(h, rows, stride=hq), :] = qv[:, h * HD : (h + 1) * HD].astype(F32)
+    for d in range(n):
+        qb[d] = qs[d * oh : (d + 1) * oh, :].astype(BF16)
     pl.semaphore_wait(barrier, n - 1 + TURNS - 1)
 
-    def spread(t, start, size, loff):
+    def spread(s):
+        t, start, size, loff = segs[s]
         return pltpu.make_async_remote_copy(
             src_ref=hidden.at[pl.ds(start, size)],
             dst_ref=hid.at[pl.ds(loff, size)],
-            send_sem=hsend.at[t],
-            recv_sem=hrecv,
+            send_sem=hsend.at[s],
+            recv_sem=hrecv.at[s],
             device_id=(p + t * prefill, c),
             device_id_type=MESH,
         )
 
     @pl.when(turn == 0)
     def _():
-        for t, start, size, loff in segs:
-            if t > 0:
-                spread(t, start, size, loff).start()
-
-    small[0].wait()
-    small[1].wait()
-    for h in range(hq):
-        qs[pl.ds(h, rows, stride=hq), :] = qv[:, h * HD : (h + 1) * HD].astype(F32)
-    for k in range(fw // HD):
-        frall[pl.ds(c, 1), k] = frv[:, k * HD : (k + 1) * HD].astype(F32)[None]
+        for s, seg in enumerate(segs):
+            if seg[0] > 0:
+                spread(s).start()
 
     def q_copy(d, slot):
         return pltpu.make_async_remote_copy(
-            src_ref=qs.at[pl.ds(pl.multiple_of(d * oh, oh), oh)],
+            src_ref=qb.at[d],
             dst_ref=qrecv.at[slot],
             send_sem=qsend.at[d],
             recv_sem=qrsem.at[slot],
@@ -154,8 +164,8 @@
 
     def f_copy(d, slot):
         return pltpu.make_async_remote_copy(
-            src_ref=frall.at[c],
-            dst_ref=frall.at[slot],
+            src_ref=fresh,
+            dst_ref=fb.at[slot],
             send_sem=fsend.at[d],
             recv_sem=frsem.at[slot],
             device_id=(g, d),
@@ -168,7 +178,7 @@
         return carry
 
     lax.fori_loop(1, n, send_q, 0)
-    qrecv[pl.ds(c, 1)] = qs[pl.ds(pl.multiple_of(c * oh, oh), oh), :][None]
+    qrecv[pl.ds(c, 1)] = qb[pl.ds(c, 1)]
 
     def rs_copy(s, d, slot):
         _, _, size, loff = segs[s]
@@ -231,11 +241,14 @@
     @pl.when(turn == 0)
     def _():
         own_hidden.wait()
-        project(0, True)
-        project(1, False)
+        for s, seg in enumerate(segs):
+            if seg[0] == 0:
+                project(s, seg[3] == 0)
 
     small[2].wait()
     for copy in small[4:]:
+        copy.wait()
+    for copy in scalars:
         copy.wait()
     for r in range(rows):
         for k in range(mkv.shape[0]):
@@ -268,8 +281,8 @@
         lp[:, k * span : (k + 1) * span] = value
         peak = jnp.maximum(peak, jnp.max(value, axis=1, keepdims=True))
     terms = jnp.sum(jnp.exp(lp[...] - peak), axis=1, keepdims=True)
-    stat[pl.ds(c, 1), 0] = jnp.broadcast_to(peak, (rows, HD))[None]
-    stat[pl.ds(c, 1), 1] = jnp.broadcast_to(terms, (rows, HD))[None]
+    side = lax.broadcasted_iota(jnp.int32, (rows, HD), 1) < HD // 2
+    stat[pl.ds(c, 1)] = jnp.where(side, peak, terms)[None]
 
     def s_copy(d, slot):
         return pltpu.make_async_remote_copy(
@@ -294,6 +307,10 @@
         return carry
 
     lax.fori_loop(1, n, recv_q, 0)
+    small[1].wait()
+    for d in range(n):
+        for k in range(fw // HD):
+            frall[d, k] = fb[d, :, k * HD : (k + 1) * HD].astype(F32)
     small[3].wait()
     position = lax.broadcasted_iota(jnp.int32, (1, npos), 1)
 
@@ -305,8 +322,10 @@
             out.append(jnp.broadcast_to(row, (GQ, HD)))
         return jnp.concatenate(out, axis=0)
 
+    arrived = [qrecv[d].astype(F32) for d in range(n)]
+    results = []
     for i in range(own):
-        query = jnp.concatenate([qrecv[d, i * hq : (i + 1) * hq, :] for d in range(n)], axis=0)
+        query = jnp.concatenate([x[i * hq : (i + 1) * hq] for x in arrived], axis=0)
         score = jnp.concatenate(
             [
                 lax.dot_general(
@@ -338,14 +357,14 @@
             ],
             axis=0,
         )
-        result = result + mine * own_rows(i, half)
-        for d in range(n):
-            osend[d, i * hq : (i + 1) * hq, :] = result[d * hq : (d + 1) * hq]
+        results.append(result + mine * own_rows(i, half))
+    for d in range(n):
+        osend[d] = jnp.concatenate([x[d * hq : (d + 1) * hq] for x in results], axis=0).astype(BF16)
 
     def o_copy(d, slot):
         return pltpu.make_async_remote_copy(
             src_ref=osend.at[d],
-            dst_ref=orecv.at[pl.ds(pl.multiple_of(slot * oh, oh), oh)],
+            dst_ref=orecv.at[slot],
             send_sem=osem.at[d],
             recv_sem=orsem.at[slot],
             device_id=(g, d),
@@ -357,20 +376,21 @@
         return carry
 
     lax.fori_loop(1, n, send_o, 0)
-    orecv[pl.ds(pl.multiple_of(c * oh, oh), oh), :] = osend[c]
+    orecv[pl.ds(c, 1)] = osend[pl.ds(c, 1)]
 
     for s, (owner, start, size, loff) in enumerate(segs):
         if owner > 0:
 
             @pl.when(turn == owner)
             def _(s=s, owner=owner, start=start, size=size, loff=loff):
-                spread(owner, start, size, loff).wait_recv()
-                project(s, True)
+                spread(s).wait_recv()
+                project(s, loff == 0)
 
     @pl.when(turn == 0)
     def _():
-        finish(0, True)
-        finish(1, False)
+        for s, seg in enumerate(segs):
+            if seg[0] == 0:
+                finish(s, seg[3] == 0)
 
     def recv_s(o, carry):
         src = peer(o)
@@ -378,17 +398,15 @@
         return carry
 
     lax.fori_loop(1, n, recv_s, 0)
-    peaks = stat[0, 0]
+    peaks = stat[0][:, :1]
     for d in range(1, n):
-        peaks = jnp.maximum(peaks, stat[d, 0])
+        peaks = jnp.maximum(peaks, stat[d][:, :1])
     total = jnp.zeros_like(peaks)
     for d in range(n):
-        total = total + stat[d, 1] * jnp.exp(stat[d, 0] - peaks)
-    norm = (peaks + jnp.log(total))[:, :1]
+        total = total + stat[d][:, HD // 2 : HD // 2 + 1] * jnp.exp(stat[d][:, :1] - peaks)
+    norm = peaks + jnp.log(total)
     value = lp[...]
     lp[...] = jnp.where(value == -jnp.inf, 0.0, value - norm)
-    lp_copy = pltpu.make_async_copy(lp, lp_out, lsem.at[2])
-    lp_copy.start()
 
     line = lax.broadcasted_iota(jnp.int32, (rows, 1), 0)
     slot = lax.rem(line, own) * n + line // own
@@ -412,8 +430,8 @@
         if owner > 0:
 
             @pl.when(turn == owner)
-            def _(s=s):
-                finish(s, True)
+            def _(s=s, loff=loff):
+                finish(s, loff == 0)
 
     def recv_o(o, carry):
         src = peer(o)
@@ -421,11 +439,13 @@
         return carry
 
     lax.fori_loop(1, n, recv_o, 0)
+    for d in range(n):
+        of[d * oh : (d + 1) * oh, :] = orecv[d].astype(F32)
 
     @pl.when(turn == 0)
     def _():
         for h in range(hq):
-            att[:, h * HD : (h + 1) * HD] = orecv[pl.ds(h, rows, stride=hq), :].astype(BF16)
+            att[:, h * HD : (h + 1) * HD] = of[pl.ds(h, rows, stride=hq), :].astype(BF16)
 
     @pl.when(turn > 0)
     def _():
@@ -469,13 +489,11 @@
             result = result + mine * mine_of(half)
             for x in range(gq):
                 h = j * gq + x
-                cached = orecv[pl.ds(h, rows, stride=hq), :]
+                cached = of[pl.ds(h, rows, stride=hq), :]
                 att[:, h * HD : (h + 1) * HD] = jnp.where(
                     landed, result[x * rows : (x + 1) * rows], cached
                 ).astype(BF16)
 
-    att_copy = pltpu.make_async_copy(att, att_out, lsem.at[0])
-    att_copy.start()
 
     def drain(o, carry):
         d = peer(o)
@@ -502,12 +520,9 @@
 
     @pl.when(turn == 0)
     def _():
-        for t, start, size, loff in segs:
-            if t > 0:
-                spread(t, start, size, loff).wait_send()
-
-    lp_copy.wait()
-    att_copy.wait()
+        for s, seg in enumerate(segs):
+            if seg[0] > 0:
+                spread(s).wait_send()
 
 
 def solution(mesh):
@@ -528,17 +543,18 @@
         ns = len(segs)
         tmax = max(size + loff for _, _, size, loff in segs)
         dma = pltpu.SemaphoreType.DMA
-        smem = pl.BlockSpec(memory_space=pltpu.SMEM)
+        vmem = pl.BlockSpec(memory_space=pltpu.VMEM)
         anys = pl.BlockSpec(memory_space=pl.ANY)
-        return pl.pallas_call(
+        made = pl.pallas_call(
             functools.partial(kernel, n, groups),
             out_shape=(
-                jax.ShapeDtypeStruct(queries.shape, BF16),
-                jax.ShapeDtypeStruct(logits.shape, F32),
+                pltpu.VMEM(queries.shape, BF16),
+                pltpu.VMEM(logits.shape, F32),
             ),
-            in_specs=[smem] * 4 + [anys] * 7,
-            out_specs=(anys, anys),
-            scratch_shapes=[
+            in_specs=[anys] * 11,
+            out_specs=(vmem, vmem),
+            scratch_shapes=[pltpu.SMEM(x.shape, jnp.int32) for x in (plen, ostep, clen, states)]
+            + [
                 pltpu.VMEM((tmax, dl), BF16),
                 pltpu.VMEM((n, dl, kw2), BF16),
                 pltpu.VMEM((n, tmax, kw2), BF16),
@@ -546,26 +562,27 @@
                 pltpu.VMEM((block, kw2), BF16),
                 pltpu.VMEM(cache.shape, BF16),
                 pltpu.VMEM(queries.shape, BF16),
-                pltpu.VMEM(fresh.shape, BF16),
+                pltpu.VMEM((n, rows, fw), BF16),
                 pltpu.VMEM(logits.shape, BF16),
                 pltpu.VMEM((masks.shape[1] // HD,) + (masks.shape[0], HD), jnp.int32),
                 pltpu.VMEM((masks.shape[1] // HD, rows, HD), jnp.int32),
                 pltpu.VMEM((rows * hq, HD), F32),
-                pltpu.VMEM((n, oh, HD), F32),
-                pltpu.VMEM((n, oh, HD), F32),
+                pltpu.VMEM((n, oh, HD), BF16),
+                pltpu.VMEM((n, oh, HD), BF16),
+                pltpu.VMEM((n, oh, HD), BF16),
+                pltpu.VMEM((n, oh, HD), BF16),
                 pltpu.VMEM((rows * hq, HD), F32),
                 pltpu.VMEM((n, fw // HD, rows, HD), F32),
-                pltpu.VMEM((n, 2, rows, HD), F32),
-                pltpu.VMEM(logits.shape, F32),
-                pltpu.VMEM(queries.shape, BF16),
+                pltpu.VMEM((n, rows, HD), F32),
                 dma((6 + masks.shape[1] // HD,)),
                 dma((n, 2)),
-                dma((TURNS,)),
-                dma,
+                dma((ns,)),
+                dma((ns,)),
                 dma((ns, n)),
                 dma((ns, n)),
                 dma((ns, TURNS)),
                 dma((ns,)),
+                dma((4,)),
                 dma((n,)),
                 dma((n,)),
                 dma((n,)),
@@ -579,6 +596,7 @@
                 collective_id=0, has_side_effects=True, vmem_limit_bytes=60 * 1024 * 1024
             ),
         )(plen, ostep, clen, states, hidden, w_kv, cache, queries, fresh, logits, masks)
+        return tuple(made)
 
     in_specs = (
         P("group", "tp"),

time: 31.1 us -> 27 us (0.87)
  the two profiles are of different devices: /device:TPU:14 before, /device:TPU:4 now
where the time goes in v2:
time: 27 us; the launch traced here: 26.9 us
  Pallas kernels  24.9 us (92%)
  local copies, waits for them, and re-layouts  1.31 us (5%)
  between operations  0.64 us (2%)
    pallas_call x1, Pallas kernels, per_device(): pl.pallas_call(functools.partial(kernel, n, groups), out_shape=(pltpu.VME...  24.9 us
    unnamed x2, local copies, waits for them, and re-layouts  1.31 us

profile of v2, /device:TPU:4, one launch (start us, length us, event | category | flops | bytes accessed | tf_op | source)
XLA Modules:
  0.0 26.9 jit_solution(9810615995216931087)
XLA Ops:
  0.6 24.9 %shard_map.122 = (bf16[8,2048]{1,0:T(8,128)(2,1)S(1)}, f32[8,7680]{1,0:T(8,128)S(1)}) custom-call(s32[2,8]{1,0:T(2,128)} %plen_in.1, s32[2,8]{1,0:T(2,128)} %ostep_in.1, s32[2]{0:T(128)} %clen_in.1, s32[8]{0:T(128)} %states_in.1, bf16[256,2048]{1,0:T(8,128)(2,1)} %hidden.1, bf16[2048,2048]{1,0:T(8,128)(2,1)} %w_kv.1, bf16[2,128,2048]{2,1,0:T(8,128)(2,1)} %cache.1, ...), custom_call_target="tpu_custom_call" | custom-call | tf_op jit(solution)/shard_map/pallas_call | solution.py:548
  25.6 0.6 %copy.15 = bf16[8,2048]{1,0:T(8,128)(2,1)} copy(bf16[8,2048]{1,0:T(8,128)(2,1)S(1)} %get-tuple-element.2) | data formatting | bytes 65536
  26.2 0.7 %copy.16 = f32[8,7680]{1,0:T(8,128)} copy(f32[8,7680]{1,0:T(8,128)S(1)} %get-tuple-element.3) | data formatting | bytes 491520

commit v3 on v2

--- a/solution.py
+++ b/solution.py
@@ -14,7 +14,7 @@
 GQ = HEADS // KVH
 TURNS = 4
 BITS = 30
-PLAN = ((0, 3), (0, 3), (1, 2), (2, 2), (3, 2), (2, 2), (1, 1), (3, 1))
+PLAN = ((0, 4), (0, 3), (3, 1), (2, 2), (3, 1), (2, 2), (1, 2), (1, 1))
 MESH = pl.DeviceIdType.MESH
 F32 = jnp.float32
 BF16 = jnp.bfloat16

time: 27 us -> 25.4 us (0.941)
  Pallas kernels: 24.9 us -> 23.3 us
    pallas_call x1, Pallas kernels: 24.9 us -> 23.3 us  [per_device(): pl.pallas_call(functools.partial(kernel, n, groups), out_shape=(pltpu.VME...]
where the time goes in v3:
time: 25.4 us; the launch traced here: 25.3 us
  Pallas kernels  23.3 us (92%)
  local copies, waits for them, and re-layouts  1.31 us (5%)
  between operations  0.64 us (3%)
    pallas_call x1, Pallas kernels, per_device(): pl.pallas_call(functools.partial(kernel, n, groups), out_shape=(pltpu.VME...  23.3 us
    unnamed x2, local copies, waits for them, and re-layouts  1.31 us

profile of v3, /device:TPU:4, one launch (start us, length us, event | category | flops | bytes accessed | tf_op | source)
XLA Modules:
  0.0 25.3 jit_solution(12247477958462865941)
XLA Ops:
  0.6 23.3 %shard_map.122 = (bf16[8,2048]{1,0:T(8,128)(2,1)S(1)}, f32[8,7680]{1,0:T(8,128)S(1)}) custom-call(s32[2,8]{1,0:T(2,128)} %plen_in.1, s32[2,8]{1,0:T(2,128)} %ostep_in.1, s32[2]{0:T(128)} %clen_in.1, s32[8]{0:T(128)} %states_in.1, bf16[256,2048]{1,0:T(8,128)(2,1)} %hidden.1, bf16[2048,2048]{1,0:T(8,128)(2,1)} %w_kv.1, bf16[2,128,2048]{2,1,0:T(8,128)(2,1)} %cache.1, ...), custom_call_target="tpu_custom_call" | custom-call | tf_op jit(solution)/shard_map/pallas_call | solution.py:548
  23.9 0.6 %copy.15 = bf16[8,2048]{1,0:T(8,128)(2,1)} copy(bf16[8,2048]{1,0:T(8,128)(2,1)S(1)} %get-tuple-element.2) | data formatting | bytes 65536
  24.6 0.7 %copy.16 = f32[8,7680]{1,0:T(8,128)} copy(f32[8,7680]{1,0:T(8,128)S(1)} %get-tuple-element.3) | data formatting | bytes 491520
